TPU v7x, 32 devices: a whole 2x2x4 slice. The times are simulated.
32 devices in a mesh: ctx: 16 (over z, x, core), fsdp: 2 (over y).
Axes of the slice: x: 2, y: 2, z: 4, core: 2. Of those that a mesh axis runs over, the one named last changes fastest.
Arguments:
- query_heads: bfloat16 [1024, 3072], P(('ctx', 'fsdp')), may hold values from -6 to 6
- kv_latent: bfloat16 [1024, 576], P(('ctx', 'fsdp')), may hold values from -800 to 800
- w_uk: bfloat16 [512, 2048], P('ctx', 'fsdp'), may hold values from -0.25 to 0.25
- w_uv: bfloat16 [512, 2048], P('ctx', 'fsdp'), may hold values from -0.25 to 0.25
- span_order: int32 [32], replicated, may hold values from 0 to 31, each once
Outputs:
- attn_out: bfloat16 [1024, 2048], P(('ctx', 'fsdp'))
Inputs may be any that keep to these rules, and one draw needn't show every extreme that they name: `span_order`: each span number appears exactly once.
All inputs are finite; a program needn't handle non-finite values.
Results may differ from a plain program's by a relative error of at most 0.01.
The roundings to bfloat16 on the way count: a program that leaves them out, or rounds other values in their place, can miss the bound.
Values may be sent and summed in bfloat16 or wider, within the bound.
A program may use at most 64 MiB of HBM per device.

v0:
```python
import math
import jax
import jax.numpy as jnp
from jax import lax
from jax.sharding import PartitionSpec as P

LATENT = 512
ROPE = 64
NOPE = 128
VDIM = 128
SPAN = 32


def lookup(entries, wanted):
    matches = wanted[:, None] == jnp.arange(entries.shape[0], dtype=jnp.int32)[None, :]
    return jnp.sum(jnp.where(matches, entries[None, :], 0), axis=1)


def position(span_order, row_ids):
    return lookup(span_order, row_ids // SPAN) * SPAN + row_ids % SPAN


def rotary_tables(position_ids):
    half_width = ROPE // 2
    frequency = 10000.0 ** (-jnp.arange(half_width, dtype=jnp.float32) / half_width)
    angles = position_ids.astype(jnp.float32)[:, None] * frequency[None, :]
    return (jnp.cos(angles), jnp.sin(angles))


def rotate(values, cos_table, sin_table):
    half_width = ROPE // 2
    values = values.astype(jnp.float32)
    first_half = values[..., :half_width]
    second_half = values[..., half_width:]
    turned = jnp.concatenate(
        [
            first_half * cos_table - second_half * sin_table,
            second_half * cos_table + first_half * sin_table,
        ],
        axis=-1,
    )
    return turned.astype(jnp.bfloat16)


def body(query_heads, kv_latent, w_uk, w_uv, span_order):
    ctx_index = lax.axis_index("ctx")
    fsdp_index = lax.axis_index("fsdp")
    fsdp_count = lax.axis_size("fsdp")
    local_count = kv_latent.shape[0]
    row_count = local_count * fsdp_count
    score_scale = 1.0 / math.sqrt(NOPE + ROPE)
    queries = lax.all_to_all(query_heads, "fsdp", split_axis=1, concat_axis=0, tiled=True)
    head_count = queries.shape[1] // (NOPE + ROPE)
    queries = queries.reshape(row_count, head_count, NOPE + ROPE)
    key_map, value_map = (
        lax.all_gather(w_uk, "ctx", axis=0, tiled=True),
        lax.all_gather(w_uv, "ctx", axis=0, tiled=True),
    )
    query_pos = position(span_order, ctx_index * row_count + jnp.arange(row_count, dtype=jnp.int32))
    own_ids = (
        ctx_index * row_count + fsdp_index * local_count + jnp.arange(local_count, dtype=jnp.int32)
    )
    own_cos, own_sin = rotary_tables(position(span_order, own_ids))
    local_keys = jnp.concatenate(
        [kv_latent[:, :LATENT], rotate(kv_latent[:, LATENT:], own_cos, own_sin)], axis=1
    )
    query_cos, query_sin = rotary_tables(query_pos)
    query_latent = jnp.einsum(
        "rhd,nhd->rhn",
        queries[:, :, :NOPE],
        key_map.reshape(LATENT, head_count, NOPE),
        preferred_element_type=jnp.float32,
    ).astype(jnp.bfloat16)
    query_rope = rotate(queries[:, :, NOPE:], query_cos[:, None, :], query_sin[:, None, :])
    query_full = jnp.concatenate([query_latent, query_rope], axis=2)
    segment = lax.all_gather(local_keys, ("ctx", "fsdp"), axis=0, tiled=True)
    key_pos = position(span_order, jnp.arange(segment.shape[0], dtype=jnp.int32))
    row_max = jnp.full((row_count, head_count), -1e30, jnp.float32)
    totals = jnp.zeros((row_count, head_count), jnp.float32)
    accum = jnp.zeros((row_count, head_count, LATENT), jnp.float32)
    seg_count = segment.shape[0]
    for sub_begin in range(0, seg_count, 1024):
        sub_keys = segment[sub_begin : sub_begin + 1024]
        sub_pos = key_pos[sub_begin : sub_begin + 1024]
        allowed = (sub_pos[None, :] <= query_pos[:, None])[:, None, :]
        score_block = (
            jnp.einsum("rhe,ke->rhk", query_full, sub_keys, preferred_element_type=jnp.float32)
            * score_scale
        )
        score_block = jnp.where(allowed, score_block, jnp.float32(-1e30))
        new_max = jnp.maximum(row_max, jnp.max(score_block, axis=2))
        exp_vals = jnp.where(allowed, jnp.exp(score_block - new_max[:, :, None]), jnp.float32(0.0))
        rescale = jnp.exp(row_max - new_max)
        totals = totals * rescale + jnp.sum(exp_vals, axis=2)
        accum = accum * rescale[:, :, None] + jnp.einsum(
            "rhk,kn->rhn",
            exp_vals.astype(jnp.bfloat16),
            sub_keys[:, :LATENT],
            preferred_element_type=jnp.float32,
        )
        row_max = new_max
    row_max, totals, accum = (row_max, totals, accum)
    out_latent = (accum / totals[:, :, None]).astype(jnp.bfloat16)
    head_out = jnp.einsum(
        "rhn,nhd->rhd",
        out_latent,
        value_map.reshape(LATENT, head_count, VDIM),
        preferred_element_type=jnp.float32,
    ).astype(jnp.bfloat16)
    head_out = head_out.reshape(row_count, head_count * VDIM)
    return lax.all_to_all(head_out, "fsdp", split_axis=0, concat_axis=1, tiled=True)


def solution(mesh):
    placed = (
        P(("ctx", "fsdp"), None),
        P(("ctx", "fsdp"), None),
        P("ctx", "fsdp"),
        P("ctx", "fsdp"),
        P(),
    )
    return jax.shard_map(
        body, mesh=mesh, in_specs=placed, out_specs=P(("ctx", "fsdp"), None), check_vma=False
    )
```

profile of v0, /device:TPU:0, one launch (start us, length us, event | category | flops | bytes accessed | tf_op | source)
XLA Modules:
  0.0 166.3 jit_solution(8451803332605785282)
XLA Ops:
  6.5 0.0 all-gather.4.cloned.1.call-start
  6.5 0.7 all-gather.4.cloned.1.call-update
  7.3 0.0 all-gather.8.cloned.1.call-start
  7.3 0.7 all-gather.8.cloned.1.call-update
  8.0 0.0 all-gather.6.cloned.1.call-start
  8.1 0.8 slice.31
  8.8 0.8 select_reduce_fusion.1
  9.7 0.7 slice_convert_fusion
  10.4 0.1 fusion.22
  10.5 0.7 pad_maximum_fusion.1
  11.2 0.0 all-gather.6.cloned.1.call-update
  11.3 1.6 copy.105
  12.9 4.2 %all-to-all-start = ((bf16[32,2,1536]{2,0,1:T(8,128)(2,1)}), bf16[32,2,1536]{2,0,1:T(8,128)(2,1)S(1)}, u32[]{:S(2)}, u32[]{:S(2)}) async-start(bf16[32,2,1536]{2,0,1:T(8,128)(2,1)} %bitcast.24), calls=%async_computation | async-start | bytes 393216 | tf_op jit(solution)/shard_map/all_to_all | solution.py:52
  17.1 0.7 select_reduce_fusion.2
  17.9 0.7 select_reduce_fusion
  18.7 0.1 broadcast_compare_fusion
  18.8 0.2 multiply_cosine_fusion
  19.0 3.3 %all-to-all-done = bf16[32,2,1536]{2,0,1:T(8,128)(2,1)S(1)} async-done(((bf16[32,2,1536]{2,0,1:T(8,128)(2,1)}), bf16[32,2,1536]{2,0,1:T(8,128)(2,1)S(1)}, u32[]{:S(2)}, u32[]{:S(2)}) %all-to-all-start) | async-done | bytes 196640 | tf_op jit(solution)/shard_map/all_to_all | solution.py:52
  22.3 0.2 reshape.213
  22.6 0.1 subtract_convert_fusion
  22.7 27.5 %all-gather.4.cloned.1.call-done = bf16[512,1024]{1,0:T(8,128)(2,1)} async-done(((bf16[32,1024]{1,0:T(8,128)(2,1)}), bf16[512,1024]{1,0:T(8,128)(2,1)}) %all-gather.4.cloned.1.call-update) | async-done | bytes 1048592 | tf_op jit(solution)/shard_map/all_gather | solution.py:56
  50.2 1.5 copy.74
  51.7 37.5 %all-gather.8.cloned.1.call-done = bf16[512,1024]{1,0:T(8,128)(2,1)} async-done(((bf16[32,1024]{1,0:T(8,128)(2,1)}), bf16[512,1024]{1,0:T(8,128)(2,1)}) %all-gather.8.cloned.1.call-update) | async-done | bytes 1048592 | tf_op jit(solution)/shard_map/all_gather | solution.py:57
  89.2 2.3 %copy.84 = bf16[512,1024]{0,1:T(8,128)(2,1)} copy(bf16[512,1024]{1,0:T(8,128)(2,1)} %all-gather.8.cloned.1.call-done) | data formatting | bytes 2097152 | tf_op jit(solution)/shard_map/all_gather | solution.py:57
  91.5 0.3 fusion.7
  91.8 0.1 pad_maximum_fusion
  91.9 53.5 %all-gather.6.cloned.1.call-done = bf16[1024,576]{1,0:T(8,128)(2,1)} async-done(((bf16[32,576]{1,0:T(8,128)(2,1)}), bf16[1024,576]{1,0:T(8,128)(2,1)}) %all-gather.6.cloned.1.call-update) | async-done | bytes 1179664 | tf_op jit(solution)/shard_map/all_gather | solution.py:76
  145.4 2.6 %fusion = (f32[64,8]{1,0:T(8,128)S(1)}, f32[64,8,1024]{2,1,0:T(8,128)S(1)}) fusion(pred[64,1024]{1,0:T(8,128)(4,1)S(1)} %broadcast_compare_fusion, bf16[1024,576]{1,0:T(8,128)(2,1)} %all-gather.6.cloned.1.call-done, bf16[64,8,576]{2,0,1:T(8,128)(2,1)S(1)} %pad_maximum_fusion), kind=kOutput, calls=%fused_computation.2 | convolution fusion | flops 605552128 | bytes 3934208 | tf_op jit(solution)/shard_map/rhe,ke->rhk/dot_general | solution.py:87
  148.1 0.1 copy.80
  148.1 0.1 copy.81
  148.2 0.8 fusion.1
  149.1 0.1 copy.83
  149.1 2.7 %fusion.10 = bf16[64,8,128]{2,0,1:T(8,128)(2,1)S(1)} fusion(bf16[512,8,128]{0,2,1:T(8,128)(2,1)} %bitcast.26, bf16[1024,576]{1,0:T(8,128)(2,1)} %all-gather.6.cloned.1.call-done, bf16[64,8,1024]{2,1,0:T(8,128)(2,1)S(1)} %get-tuple-element.8, f32[64,8]{0,1:T(8,128)S(1)} %get-tuple-element.14, f32[64,8]{0,1:T(8,128)S(1)} %get-tuple-element.13), kind=kOutput, calls=%fused_computation.14 | convolution fusion | flops 604831744 | bytes 3280896 | tf_op jit(solution)/shard_map/rhn,nhd->rhd/dot_general | solution.py:104
  151.9 0.1 copy.86
  152.0 0.1 all_to_all.29
  152.1 7.0 %all_to_all.35 = bf16[2,32,1024]{2,1,0:T(8,128)(2,1)S(1)} all-to-all(bf16[2,32,1024]{2,1,0:T(8,128)(2,1)S(1)} %all_to_all.29), channel_id=1, replica_groups=mesh['ctx'=16,'fsdp'=2] {'fsdp'}, dimensions={0} | all-to-all | bytes 262144 | tf_op jit(solution)/shard_map/all_to_all | solution.py:111
  159.1 0.7 copy.93
  (12 shorter events, 0.1 us)
Async XLA Ops:
  6.5 43.7 %all-gather.4.cloned.1.call-start = ((), (), s32[]{:S(2)}) async-start(), calls=%async_computation.2 | async-start | bytes 1114112 | tf_op jit(solution)/shard_map/all_gather | solution.py:56
  7.3 82.0 %all-gather.8.cloned.1.call-start = ((), (), s32[]{:S(2)}) async-start(), calls=%async_computation.4 | async-start | bytes 1114112 | tf_op jit(solution)/shard_map/all_gather | solution.py:57
  8.0 137.4 %all-gather.6.cloned.1.call-start = ((), (), s32[]{:S(2)}) async-start(), calls=%async_computation.3 | async-start | bytes 1351680 | tf_op jit(solution)/shard_map/all_gather | solution.py:76
  12.9 9.4 %all-to-all-start = ((bf16[32,2,1536]{2,0,1:T(8,128)(2,1)}), bf16[32,2,1536]{2,0,1:T(8,128)(2,1)S(1)}, u32[]{:S(2)}, u32[]{:S(2)}) async-start(bf16[32,2,1536]{2,0,1:T(8,128)(2,1)} %bitcast.24), calls=%async_computation | async-start | bytes 393216 | tf_op jit(solution)/shard_map/all_to_all | solution.py:52
Sparse Core Ops, SparseCore 0:
  9.5 40.6 all-gather.3
  52.3 36.8 all-gather.7
  92.1 53.3 all-gather.5
where the time goes:
time: 167 us; the launch traced here: 166 us
  waiting for transfers between devices  123 us (74%)
  between operations  13.2 us (8%)
  local copies, waits for them, and re-layouts  7.41 us (4%)
  blocking collectives  7.04 us (4%)
  matrix products  5.68 us (3%)
  other arithmetic  5.37 us (3%)
  starting transfers between devices  4.31 us (3%)
    all_gather x1, waiting for transfers between devices, body(): segment = lax.all_gather(local_keys, ('ctx', 'fsdp'), axis=0, tiled=True)  53.5 us
    all_gather x1, waiting for transfers between devices, body(): lax.all_gather(w_uv, 'ctx', axis=0, tiled=True)  37.5 us
    all_gather x1, waiting for transfers between devices, body(): lax.all_gather(w_uk, 'ctx', axis=0, tiled=True)  27.5 us
    all_to_all x1, blocking collectives, body(): lax.all_to_all(head_out, 'fsdp', split_axis=0, concat_axis=1, tiled=True)  7.04 us
    all_to_all x1, starting transfers between devices, body(): lax.all_to_all(query_heads, 'fsdp', split_axis=1, concat_axis=0, tiled=True)  4.23 us
  transfers between devices with their start and end apart: 4, of which 4 were waited for; matrix products, arithmetic and copies ran while one was open for 7% of the time, Pallas kernels for 0%

commit v1 on v0

--- a/solution.py
+++ b/solution.py
@@ -9,6 +9,36 @@
 NOPE = 128
 VDIM = 128
 SPAN = 32
+
+
+def see_rates_all(a0, at_axis):
+    a0 = jnp.moveaxis(a0, 0, at_axis)
+    current_arr = a0.shape
+    return a0.reshape(
+        *current_arr[:at_axis],
+        current_arr[at_axis] * current_arr[at_axis + 1],
+        *current_arr[at_axis + 2 :]
+    )
+
+
+def _check_tracks(w_in, along_axis):
+    next_value = lax.axis_size(along_axis)
+    val2, moved = (next_value, lax.axis_index(along_axis))
+    part_next, plain = (w_in[None], 1)
+    while plain < val2:
+        mid_arr = lax.ppermute(
+            part_next, along_axis, perm=[(to_i, to_i ^ plain) for to_i in range(val2)]
+        )
+        all_values = moved & plain == 0
+        part_next = jnp.concatenate(
+            [jnp.where(all_values, part_next, mid_arr), jnp.where(all_values, mid_arr, part_next)]
+        )
+        plain *= 2
+    return part_next
+
+
+def read_slabs(payload, slab_in, dim_no):
+    return see_rates_all(_check_tracks(payload, slab_in), dim_no)
 
 
 def lookup(entries, wanted):
@@ -53,7 +83,7 @@
     head_count = queries.shape[1] // (NOPE + ROPE)
     queries = queries.reshape(row_count, head_count, NOPE + ROPE)
     key_map, value_map = (
-        lax.all_gather(w_uk, "ctx", axis=0, tiled=True),
+        read_slabs(w_uk, "ctx", 0),
         lax.all_gather(w_uv, "ctx", axis=0, tiled=True),
     )
     query_pos = position(span_order, ctx_index * row_count + jnp.arange(row_count, dtype=jnp.int32))

time: 167 us -> 145 us (0.87)
  waiting for transfers between devices: 123 us -> 93.5 us
  starting transfers between devices: 4.31 us -> 10.8 us
    ppermute x0 -> x4, waiting for transfers between devices: none -> 37.7 us  [_check_tracks(): lax.ppermute(part_next, along_axis, perm=[(to_i, to_i ^ plain) for to_i i...]
    all_gather x1, waiting for transfers between devices: 37.5 us -> 0.02 us  [body(): lax.all_gather(w_uv, 'ctx', axis=0, tiled=True)]
    all_gather x1 -> x0, waiting for transfers between devices: 27.5 us -> none  [body(): lax.all_gather(w_uk, 'ctx', axis=0, tiled=True)]
    ppermute x0 -> x4, starting transfers between devices: none -> 7.05 us  [_check_tracks(): lax.ppermute(part_next, along_axis, perm=[(to_i, to_i ^ plain) for to_i i...]
    all_to_all x1, waiting for transfers between devices: 3.3 us -> 0.01 us  [body(): lax.all_to_all(query_heads, 'fsdp', split_axis=1, concat_axis=0, tiled=True)]
  transfers between devices with their start and end apart: 4 -> 7, of which waited for: 4 -> 4; matrix products, arithmetic and copies ran while one was open for 7% -> 8% of each run, Pallas kernels for 0% -> 0%
where the time goes in v1:
time: 145 us; the launch traced here: 144 us
  waiting for transfers between devices  93.5 us (64%)
  between operations  13.6 us (9%)
  starting transfers between devices  10.8 us (7%)
  blocking collectives  7.05 us (5%)
  local copies, waits for them, and re-layouts  6.8 us (5%)
  other arithmetic  6.54 us (5%)
  matrix products  5.78 us (4%)
    all_gather x1, waiting for transfers between devices, body(): segment = lax.all_gather(local_keys, ('ctx', 'fsdp'), axis=0, tiled=True)  55 us
    ppermute x4, waiting for transfers between devices, _check_tracks(): lax.ppermute(part_next, along_axis, perm=[(to_i, to_i ^ plain) for to_i i...  37.7 us
    all_to_all x1, blocking collectives, body(): lax.all_to_all(head_out, 'fsdp', split_axis=0, concat_axis=1, tiled=True)  7.05 us
    ppermute x4, starting transfers between devices, _check_tracks(): lax.ppermute(part_next, along_axis, perm=[(to_i, to_i ^ plain) for to_i i...  7.05 us
    all_to_all x1, starting transfers between devices, body(): lax.all_to_all(query_heads, 'fsdp', split_axis=1, concat_axis=0, tiled=True)  3.8 us
  transfers between devices with their start and end apart: 7, of which 4 were waited for; matrix products, arithmetic and copies ran while one was open for 8% of the time, Pallas kernels for 0%

profile of v1, /device:TPU:0, one launch (start us, length us, event | category | flops | bytes accessed | tf_op | source)
XLA Modules:
  0.0 144.1 jit_solution(7762876091349842358)
XLA Ops:
  6.5 0.0 all-gather.5.cloned.1.call-start
  6.5 0.7 all-gather.5.cloned.1.call-update
  7.3 0.5 collective-permute-start
  7.8 1.6 %copy.102 = bf16[4,2,8,1536]{3,2,0,1:T(8,128)(2,1)} copy(bf16[4,2,8,1536]{3,2,1,0:T(8,128)(2,1)} %bitcast.34) | data formatting | bytes 393216 | tf_op jit(solution)/shard_map/all_to_all | solution.py:82
  9.4 3.8 %all-to-all-start = ((bf16[32,2,1536]{2,0,1:T(8,128)(2,1)}), bf16[32,2,1536]{2,0,1:T(8,128)(2,1)S(1)}, u32[]{:S(2)}, u32[]{:S(2)}) async-start(bf16[32,2,1536]{2,0,1:T(8,128)(2,1)} %bitcast.28), calls=%async_computation | async-start | bytes 393216 | tf_op jit(solution)/shard_map/all_to_all | solution.py:82
  13.2 0.0 all-gather.3.cloned.1.call-start
  13.2 0.8 slice.31
  14.0 0.8 select_reduce_fusion.1
  14.8 0.7 slice_convert_fusion
  15.5 0.1 fusion.23
  15.7 0.7 pad_maximum_fusion.5
  16.4 0.0 all-gather.3.cloned.1.call-update
  16.4 0.7 select_reduce_fusion
  17.2 0.0 collective-permute-done
  17.2 0.9 broadcast_select_fusion.7
  18.1 2.3 %collective-permute-start.1 = (bf16[2,32,1024]{2,1,0:T(8,128)(2,1)S(1)}, bf16[2,32,1024]{2,1,0:T(8,128)(2,1)S(1)}, u32[]{:S(2)}, u32[]{:S(2)}) collective-permute-start(bf16[2,32,1024]{2,1,0:T(8,128)(2,1)S(1)} %pad_maximum_fusion.4), channel_id=1, source_target_pairs={{0,4},{2,6},{4,0},{6,2},{8,12},{10,14},{12,8},{14,10},{16,20},{18,... | collective-permute-start | bytes 393224 | tf_op jit(solution)/shard_map/ppermute | solution.py:29
  20.3 0.7 select_reduce_fusion.2
  21.1 4.1 %collective-permute-done.1 = bf16[2,32,1024]{2,1,0:T(8,128)(2,1)S(1)} collective-permute-done((bf16[2,32,1024]{2,1,0:T(8,128)(2,1)S(1)}, bf16[2,32,1024]{2,1,0:T(8,128)(2,1)S(1)}, u32[]{:S(2)}, u32[]{:S(2)}) %collective-permute-start.1) | collective-permute-done | bytes 131104 | tf_op jit(solution)/shard_map/ppermute | solution.py:29
  25.2 1.9 %collective-permute-start.2 = (bf16[4,32,1024]{2,1,0:T(8,128)(2,1)S(1)}, bf16[4,32,1024]{2,1,0:T(8,128)(2,1)S(1)}, u32[]{:S(2)}, u32[]{:S(2)}) collective-permute-start(bf16[4,32,1024]{2,1,0:T(8,128)(2,1)S(1)} %pad_maximum_fusion.3), channel_id=1, source_target_pairs={{0,8},{2,10},{4,12},{6,14},{8,0},{10,2},{12,4},{14,6},{16,24},{18,... | collective-permute-start | bytes 786440 | tf_op jit(solution)/shard_map/ppermute | solution.py:29
  27.2 0.1 broadcast_compare_fusion
  27.3 7.1 %collective-permute-done.2 = bf16[4,32,1024]{2,1,0:T(8,128)(2,1)S(1)} collective-permute-done((bf16[4,32,1024]{2,1,0:T(8,128)(2,1)S(1)}, bf16[4,32,1024]{2,1,0:T(8,128)(2,1)S(1)}, u32[]{:S(2)}, u32[]{:S(2)}) %collective-permute-start.2) | collective-permute-done | bytes 262176 | tf_op jit(solution)/shard_map/ppermute | solution.py:29
  34.4 2.4 %collective-permute-start.3 = (bf16[8,32,1024]{2,1,0:T(8,128)(2,1)S(1)}, bf16[8,32,1024]{2,1,0:T(8,128)(2,1)S(1)}, u32[]{:S(2)}, u32[]{:S(2)}) collective-permute-start(bf16[8,32,1024]{2,1,0:T(8,128)(2,1)S(1)} %pad_maximum_fusion.2), channel_id=1, source_target_pairs={{0,16},{2,18},{4,20},{6,22},{8,24},{10,26},{12,28},{14,30},{16,0},... | collective-permute-start | bytes 1572872 | tf_op jit(solution)/shard_map/ppermute | solution.py:29
  36.8 0.2 multiply_cosine_fusion
  37.0 0.0 all-to-all-done
  37.0 0.2 reshape.209
  37.3 0.0 copy-start
  37.3 0.1 subtract_convert_fusion
  37.5 26.6 %collective-permute-done.3 = bf16[8,32,1024]{2,1,0:T(8,128)(2,1)S(1)} collective-permute-done((bf16[8,32,1024]{2,1,0:T(8,128)(2,1)S(1)}, bf16[8,32,1024]{2,1,0:T(8,128)(2,1)S(1)}, u32[]{:S(2)}, u32[]{:S(2)}) %collective-permute-start.3) | collective-permute-done | bytes 524320 | tf_op jit(solution)/shard_map/ppermute | solution.py:29
  64.0 0.1 broadcast_select_fusion.1
  64.1 0.1 pad_maximum_fusion
  64.2 0.0 slice-start
  64.2 0.3 copy.88
  64.5 0.6 slice-done
  65.1 0.5 fusion.7
  65.6 0.1 pad_maximum_fusion.1
  65.7 0.0 all-gather.5.cloned.1.call-done
  65.8 2.3 %copy.79 = bf16[512,1024]{0,1:T(8,128)(2,1)} copy(bf16[512,1024]{1,0:T(8,128)(2,1)} %all-gather.5.cloned.1.call-done) | data formatting | bytes 2097152 | tf_op jit(solution)/shard_map/all_gather | solution.py:87
  68.1 55.0 %all-gather.3.cloned.1.call-done = bf16[1024,576]{1,0:T(8,128)(2,1)} async-done(((bf16[32,576]{1,0:T(8,128)(2,1)}), bf16[1024,576]{1,0:T(8,128)(2,1)}) %all-gather.3.cloned.1.call-update) | async-done | bytes 1179664 | tf_op jit(solution)/shard_map/all_gather | solution.py:106
  123.0 2.6 %fusion = (f32[64,8]{1,0:T(8,128)S(1)}, f32[64,8,1024]{2,1,0:T(8,128)S(1)}) fusion(pred[64,1024]{1,0:T(8,128)(4,1)S(1)} %broadcast_compare_fusion, bf16[1024,576]{1,0:T(8,128)(2,1)} %all-gather.3.cloned.1.call-done, bf16[64,8,576]{2,0,1:T(8,128)(2,1)S(1)} %pad_maximum_fusion.1), kind=kOutput, calls=%fused_computation.2 | convolution fusion | flops 605552128 | bytes 3934208 | tf_op jit(solution)/shard_map/rhe,ke->rhk/dot_general | solution.py:117
  125.7 0.1 copy.75
  125.7 0.1 copy.76
  125.8 0.8 fusion.1
  126.6 0.1 copy.78
  126.7 2.7 %fusion.10 = bf16[64,8,128]{2,0,1:T(8,128)(2,1)S(1)} fusion(bf16[512,8,128]{0,2,1:T(8,128)(2,1)} %bitcast.30, bf16[1024,576]{1,0:T(8,128)(2,1)} %all-gather.3.cloned.1.call-done, bf16[64,8,1024]{2,1,0:T(8,128)(2,1)S(1)} %get-tuple-element.8, f32[64,8]{0,1:T(8,128)S(1)} %get-tuple-element.22, f32[64,8]{0,1:T(8,128)S(1)} %get-tuple-element.21), kind=kOutput, calls=%fused_computation.14 | convolution fusion | flops 604831744 | bytes 3280896 | tf_op jit(solution)/shard_map/rhn,nhd->rhd/dot_general | solution.py:134
  129.4 0.1 copy.81
  129.5 0.1 all_to_all.29
  129.6 7.0 %all_to_all.35 = bf16[2,32,1024]{2,1,0:T(8,128)(2,1)S(1)} all-to-all(bf16[2,32,1024]{2,1,0:T(8,128)(2,1)S(1)} %all_to_all.29), channel_id=1, replica_groups=mesh['ctx'=16,'fsdp'=2] {'fsdp'}, dimensions={0} | all-to-all | bytes 262144 | tf_op jit(solution)/shard_map/all_to_all | solution.py:141
  136.6 0.7 copy.87
  (17 shorter events, 0.3 us)
Async XLA Ops:
  6.5 59.2 %all-gather.5.cloned.1.call-start = ((), (), s32[]{:S(2)}) async-start(), calls=%async_computation.3 | async-start | bytes 1114112 | tf_op jit(solution)/shard_map/all_gather | solution.py:87
  7.3 9.9 %collective-permute-start = (bf16[1,32,1024]{2,1,0:T(8,128)(2,1)}, bf16[1,32,1024]{2,1,0:T(8,128)(2,1)S(1)}, u32[]{:S(2)}, u32[]{:S(2)}) collective-permute-start(bf16[1,32,1024]{2,1,0:T(8,128)(2,1)} %bitcast.35), channel_id=1, source_target_pairs={{0,2},{2,0},{4,6},{6,4},{8,10},{10,8},{12,14},{14,12},{16,18},{18,... | collective-permute-start | bytes 196616 | tf_op jit(solution)/shard_map/ppermute | solution.py:29
  9.4 27.6 %all-to-all-start = ((bf16[32,2,1536]{2,0,1:T(8,128)(2,1)}), bf16[32,2,1536]{2,0,1:T(8,128)(2,1)S(1)}, u32[]{:S(2)}, u32[]{:S(2)}) async-start(bf16[32,2,1536]{2,0,1:T(8,128)(2,1)} %bitcast.28), calls=%async_computation | async-start | bytes 393216 | tf_op jit(solution)/shard_map/all_to_all | solution.py:82
  13.2 109.9 %all-gather.3.cloned.1.call-start = ((), (), s32[]{:S(2)}) async-start(), calls=%async_computation.2 | async-start | bytes 1351680 | tf_op jit(solution)/shard_map/all_gather | solution.py:106
  18.1 7.1 %collective-permute-start.1 = (bf16[2,32,1024]{2,1,0:T(8,128)(2,1)S(1)}, bf16[2,32,1024]{2,1,0:T(8,128)(2,1)S(1)}, u32[]{:S(2)}, u32[]{:S(2)}) collective-permute-start(bf16[2,32,1024]{2,1,0:T(8,128)(2,1)S(1)} %pad_maximum_fusion.4), channel_id=1, source_target_pairs={{0,4},{2,6},{4,0},{6,2},{8,12},{10,14},{12,8},{14,10},{16,20},{18,... | collective-permute-start | bytes 393224 | tf_op jit(solution)/shard_map/ppermute | solution.py:29
  25.2 9.1 %collective-permute-start.2 = (bf16[4,32,1024]{2,1,0:T(8,128)(2,1)S(1)}, bf16[4,32,1024]{2,1,0:T(8,128)(2,1)S(1)}, u32[]{:S(2)}, u32[]{:S(2)}) collective-permute-start(bf16[4,32,1024]{2,1,0:T(8,128)(2,1)S(1)} %pad_maximum_fusion.3), channel_id=1, source_target_pairs={{0,8},{2,10},{4,12},{6,14},{8,0},{10,2},{12,4},{14,6},{16,24},{18,... | collective-permute-start | bytes 786440 | tf_op jit(solution)/shard_map/ppermute | solution.py:29
  34.4 29.6 %collective-permute-start.3 = (bf16[8,32,1024]{2,1,0:T(8,128)(2,1)S(1)}, bf16[8,32,1024]{2,1,0:T(8,128)(2,1)S(1)}, u32[]{:S(2)}, u32[]{:S(2)}) collective-permute-start(bf16[8,32,1024]{2,1,0:T(8,128)(2,1)S(1)} %pad_maximum_fusion.2), channel_id=1, source_target_pairs={{0,16},{2,18},{4,20},{6,22},{8,24},{10,26},{12,28},{14,30},{16,0},... | collective-permute-start | bytes 1572872 | tf_op jit(solution)/shard_map/ppermute | solution.py:29
  37.3 27.0 %copy-start = (bf16[64,8,192]{2,1,0:T(8,128)(2,1)}, bf16[64,8,192]{2,1,0:T(8,128)(2,1)S(1)}, u32[]{:S(2)}) copy-start(bf16[64,8,192]{2,1,0:T(8,128)(2,1)S(1)} %reshape.209) | copy-start | bytes 589828
  64.2 0.9 slice-start
Sparse Core Ops, SparseCore 0:
  9.5 56.1 all-gather.4
  68.6 54.4 all-gather.2
